TPU v7x, 32 devices: a whole 2x2x4 slice. The times are simulated.
32 devices in a mesh: store: 8 (over z, y), tensor: 4 (over x, core).
Axes of the slice: x: 2, y: 2, z: 4, core: 2. Of those that a mesh axis runs over, the one named last changes fastest.
Arguments:
- tokens: bfloat16 [8192, 8192], P('store', 'tensor'), may hold values from -1200 to 1200
- norm_gain: float32 [8192], P('tensor'), may hold values from 0.1 to 1.9
- kv_weight: bfloat16 [8192, 2, 1024], P('tensor'), may hold values from -0.0625 to 0.0625
- adapter_down: bfloat16 [32, 8192, 128], P('store', 'tensor'), may hold values from -0.0625 to 0.0625
- adapter_up: bfloat16 [32, 2, 64, 1024], P('store', None, None, 'tensor'), may hold values from -0.75 to 0.75
- token_adapters: int32 [8192, 1], P('store'), may hold values from 0 to 31; in each aligned block of 1024 rows (0 to 1023, 1024 to 2047, ...) at most 40 rows name the same one
- adapter_slot: int32 [32], replicated, may hold values from 0 to 31, each once
- request_lengths: int32 [16], replicated, may hold values from 1 to 4096, 8192 in all
Outputs:
- new_keys: bfloat16 [8192, 1024], P('store', 'tensor')
- new_values: bfloat16 [8192, 1024], P('store', 'tensor')
Inputs may be any that keep to these rules, and one draw needn't show every extreme that they name: `token_adapters`: among the 1024 tokens of one index of store no adapter is named more than 40 times; in every draw some adapter is named exactly 40 times by the tokens of some index. `adapter_slot`: each row 0 to 31 appears once. `request_lengths`: the lengths sum to 8192; the largest is exactly 4096.
All inputs are finite; a program needn't handle non-finite values.
Results may differ from a plain program's by a relative error of at most 0.0061.
Values may be sent and summed in bfloat16 or wider, within the bound.
A program may use at most 128 MiB of HBM per device.

v0:
```python
import math
import jax
import jax.numpy as jnp
from jax import lax
from jax.sharding import PartitionSpec as P

D = 8192
HEAD = 128
ADAPTER_RANK = 64
epsilon = 1e-05
adapter_scale = 2.0
rope_theta = 500000.0


def place_rows(adapter_ids, adapter_slot, capacity):
    catalog = jnp.arange(adapter_slot.shape[0], dtype=jnp.int32)
    slot_rows = jnp.sum(
        jnp.where(adapter_ids[:, None] == catalog[None, :], adapter_slot[None, :], 0), axis=1
    )
    row_order = jnp.arange(adapter_ids.shape[0], dtype=jnp.int32)
    same_earlier = (adapter_ids[:, None] == adapter_ids[None, :]) & (
        row_order[None, :] < row_order[:, None]
    )
    rank_rows = jnp.sum(same_earlier.astype(jnp.int32), axis=1)
    return slot_rows * capacity + rank_rows


def positions_of(first_row, row_count, lengths):
    global_rows = first_row + jnp.arange(row_count, dtype=jnp.int32)
    request_ends = jnp.cumsum(lengths)
    preceding = jnp.sum(
        jnp.where(request_ends[None, :] <= global_rows[:, None], lengths[None, :], 0), axis=1
    )
    return global_rows - preceding


def rotate(states, positions):
    per_head = states.reshape(states.shape[0], -1, HEAD)
    half_size = HEAD // 2
    frequency = jnp.exp(
        jnp.arange(half_size, dtype=jnp.float32) * (-2.0 * math.log(rope_theta) / HEAD)
    )
    angles = positions.astype(jnp.float32)[:, None] * frequency[None, :]
    cos_part = jnp.concatenate([jnp.cos(angles), jnp.cos(angles)], axis=1)[:, None, :]
    sin_part = jnp.concatenate([jnp.sin(angles), jnp.sin(angles)], axis=1)[:, None, :]
    low_half = per_head[..., :half_size]
    high_half = per_head[..., half_size:]
    turned = jnp.concatenate([-high_half, low_half], axis=-1)
    return (per_head * cos_part + turned * sin_part).reshape(states.shape)


def local(
    tokens,
    norm_gain,
    kv_weight,
    adapter_down,
    adapter_up,
    token_adapters,
    adapter_slot,
    request_lengths,
):
    row_count = tokens.shape[0]
    local_width = tokens.shape[1]
    adapter_total = adapter_slot.shape[0]
    capacity = max(2, 5 * row_count // (4 * adapter_total))
    store_size = lax.axis_size("store")
    per_owner = adapter_down.shape[0]
    kv_local = adapter_up.shape[3]
    widened = tokens.astype(jnp.float32)
    squares = lax.psum(jnp.sum(widened * widened, axis=1), "tensor")
    normed = (widened * lax.rsqrt(squares / D + epsilon)[:, None] * norm_gain[None, :]).astype(
        jnp.bfloat16
    )
    targets = place_rows(token_adapters[:, 0], adapter_slot, capacity)
    send_rows = (
        jnp.zeros((adapter_total * capacity, local_width), jnp.bfloat16).at[targets].set(normed)
    )
    send_rows = send_rows.reshape(store_size, per_owner, capacity, local_width)
    down_projected = jnp.einsum(
        "slcd,ldr->slcr",
        lax.all_to_all(send_rows, "store", split_axis=0, concat_axis=0, tiled=True),
        adapter_down,
        preferred_element_type=jnp.float32,
    )
    rank_total_sum = lax.psum(down_projected, "tensor")
    rank_activation = (rank_total_sum * adapter_scale).astype(jnp.bfloat16)
    split_rank = rank_activation.reshape(rank_activation.shape[:3] + (2, ADAPTER_RANK))
    update_rows = jnp.einsum(
        "slcjr,ljrk->slcjk", split_rank, adapter_up, preferred_element_type=jnp.float32
    )
    back_rows = update_rows.astype(jnp.bfloat16).reshape(
        rank_activation.shape[:3] + (2 * kv_local,)
    )
    returned = lax.all_to_all(back_rows, "store", split_axis=0, concat_axis=0, tiled=True)
    delta_rows = returned.reshape(adapter_total * capacity, 2, kv_local)[targets]
    partial_value = jnp.einsum("td,djk->tjk", normed, kv_weight, preferred_element_type=jnp.float32)
    base_part = lax.psum_scatter(partial_value, "tensor", scatter_dimension=2, tiled=True)
    combined = base_part + delta_rows.astype(jnp.float32)
    positions = positions_of(lax.axis_index("store") * row_count, row_count, request_lengths)
    new_keys = rotate(combined[:, 0, :], positions).astype(jnp.bfloat16)
    new_values = combined[:, 1, :].astype(jnp.bfloat16)
    return (new_keys, new_values)


def solution(mesh):
    return jax.shard_map(
        local,
        mesh=mesh,
        in_specs=(
            P("store", "tensor"),
            P("tensor"),
            P("tensor", None, None),
            P("store", "tensor", None),
            P("store", None, None, "tensor"),
            P("store", None),
            P(),
            P(),
        ),
        out_specs=(P("store", "tensor"), P("store", "tensor")),
        check_vma=False,
    )
```

profile of v0, /device:TPU:0, one launch (start us, length us, event | category | flops | bytes accessed | tf_op | source)
XLA Modules:
  0.0 278.7 jit_solution(12801032871038219586)
XLA Ops:
  7.2 1.4 convert_reduce_fusion
  8.6 0.8 select_reduce_fusion
  9.4 3.1 %fusion = f32[1024]{0:T(1024)S(1)} fusion(bf16[1024,2048]{1,0:T(8,128)(2,1)} %param.8), kind=kLoop, calls=%fused_computation.4 | loop fusion | flops 6290432 | bytes 4198400 | tf_op jit(solution)/shard_map/reduce_sum | solution.py:70
  12.5 8.4 %psum.14 = f32[1024]{0:T(1024)S(1)} all-reduce(f32[1024]{0:T(1024)S(1)} %fusion), channel_id=1, replica_groups=mesh['store'=8,'tensor'=4] {'tensor'}, use_global_device_ids=true, to_apply=%region_1.0 | all-reduce | flops 1024 | bytes 8192 | tf_op jit(solution)/shard_map/psum | solution.py:70
  20.9 11.2 %scatter_custom_fusion = bf16[1280,2048]{1,0:T(8,128)(2,1)} fusion(s32[1024]{0:T(1024)S(1)} %bitcast.50, bf16[]{:T(256)} %constant.6.clone.1, bf16[1024,2048]{1,0:T(8,128)(2,1)} %param.8, f32[2048]{0:T(1024)S(1)} %copy-done.6, f32[1024]{0:T(1024)S(1)} %add_rsqrt_fusion), kind=kCustom, calls=%fused_computation.15 | custom fusion | flops 8388608 | bytes 9449474 | tf_op jit(solution)/shard_map/scatter | solution.py:76
  32.1 120.3 %all_to_all.10 = bf16[8,4,40,2048]{3,2,1,0:T(8,128)(2,1)S(1)} all-to-all(bf16[8,4,40,2048]{3,2,1,0:T(8,128)(2,1)} %bitcast.46), channel_id=1, replica_groups=mesh['store'=8,'tensor'=4] {'store'}, dimensions={0} | all-to-all | bytes 10485760 | tf_op jit(solution)/shard_map/all_to_all | solution.py:81
  152.4 2.5 fusion.13
  154.9 0.2 reduce-scatter.2.cloned.1.call-start
  155.1 14.9 %fusion.3 = f32[1024,2,1024]{2,0,1:T(8,128)} fusion(bf16[2048,2,1024]{2,1,0:T(2,128)(2,1)} %param.10, bf16[1024,2048]{1,0:T(8,128)(2,1)} %param.8, f32[2048]{0:T(1024)S(1)} %copy-done.6, f32[1024]{0:T(1024)S(1)} %add_rsqrt_fusion), kind=kOutput, calls=%fused_computation.7 | convolution fusion | flops 8598323200 | bytes 20983808 | tf_op jit(solution)/shard_map/td,djk->tjk/dot_general | solution.py:96
  170.0 18.1 %all-reduce.2.cloned.1.call-done = f32[8,4,40,128]{3,2,0,1:T(8,128)} async-done(((f32[8,4,40,128]{3,2,0,1:T(8,128)}), f32[8,4,40,128]{3,2,0,1:T(8,128)}) %all-reduce.2.cloned.1.call-update) | async-done | bytes 655376 | tf_op jit(solution)/shard_map/psum | solution.py:85
  188.1 1.1 multiply_convert_fusion
  189.3 0.3 reshape.96
  189.6 0.5 fusion.12
  190.1 1.3 copy.28
  191.5 1.7 reshape.97
  193.2 5.5 %all-to-all-start.1 = ((bf16[8,4,40,512]{3,2,1,0:T(8,128)(2,1)}), bf16[8,4,40,512]{3,2,1,0:T(8,128)(2,1)S(1)}, u32[]{:S(2)}, u32[]{:S(2)}) async-start(bf16[8,4,40,512]{3,2,1,0:T(8,128)(2,1)} %reshape.97), calls=%async_computation.2 | async-start | bytes 2621440 | tf_op jit(solution)/shard_map/all_to_all | solution.py:94
  198.8 0.1 reduce
  199.0 1.9 multiply_cosine_fusion
  200.9 1.3 pad_maximum_fusion
  202.2 27.2 %all-to-all-done.1 = bf16[8,4,40,512]{3,2,1,0:T(8,128)(2,1)S(1)} async-done(((bf16[8,4,40,512]{3,2,1,0:T(8,128)(2,1)}), bf16[8,4,40,512]{3,2,1,0:T(8,128)(2,1)S(1)}, u32[]{:S(2)}, u32[]{:S(2)}) %all-to-all-start.1) | async-done | bytes 1310752 | tf_op jit(solution)/shard_map/all_to_all | solution.py:94
  229.4 1.2 reshape.98
  230.6 5.5 %gather_fusion = bf16[1024,2,256]{2,1,0:T(2,128)(2,1)S(1)} fusion(bf16[1280,2,256]{2,1,0:T(2,128)(2,1)} %reshape.98, s32[1024]{0:T(1024)S(1)} %broadcast_clamp_fusion), kind=kCustom, calls=%fused_computation | custom fusion | bytes 2101248 | tf_op jit(solution)/shard_map/gather | solution.py:95
  236.1 25.9 %reduce-scatter.2.cloned.1.call-done = f32[1024,2,256]{2,0,1:T(8,128)} async-done(((f32[1024,2,1024]{2,0,1:T(8,128)}), f32[1024,2,256]{2,0,1:T(8,128)}) %reduce-scatter.2.cloned.1.call-update) | async-done | bytes 2097168 | tf_op jit(solution)/shard_map/reduce_scatter | solution.py:97
  262.0 1.8 convert_add_fusion
  263.8 1.1 slice.19
  264.9 0.5 copy-done.1
  265.5 0.8 fusion.22
  266.3 1.7 reshape_squeeze.6
  268.1 1.1 slice_negate_fusion
  269.3 1.2 maximum_multiply_fusion
  270.5 0.4 mul.103
  270.9 1.0 fusion.20
  (28 shorter events, 0.4 us)
Async XLA Ops:
  7.2 145.2 %copy-start = (bf16[4,2048,128]{2,1,0:T(8,128)(2,1)S(1)}, bf16[4,2048,128]{2,1,0:T(8,128)(2,1)}, u32[]{:S(2)}) copy-start(bf16[4,2048,128]{2,1,0:T(8,128)(2,1)} %param.11) | copy-start | bytes 6291460
  7.2 13.7 %copy-start.6 = (f32[2048]{0:T(1024)S(1)}, f32[2048]{0:T(1024)}, u32[]{:S(2)}) copy-start(f32[2048]{0:T(1024)} %param.9) | copy-start | bytes 24580
  7.2 180.9 %all-reduce.2.cloned.1.call-start = ((), (), s32[]{:S(2)}) async-start(), calls=%async_computation.4 | async-start | bytes 1310720 | tf_op jit(solution)/shard_map/psum | solution.py:85
  154.9 107.1 %reduce-scatter.2.cloned.1.call-start = ((), (), s32[]{:S(2)}) async-start(), calls=%async_computation.3 | async-start | bytes 10485760 | tf_op jit(solution)/shard_map/reduce_scatter | solution.py:97
  170.0 19.6 %copy-start.5 = (bf16[4,2,64,256]{3,2,1,0:T(8,128)(2,1)S(1)}, bf16[4,2,64,256]{3,2,1,0:T(8,128)(2,1)}, u32[]{:S(2)}) copy-start(bf16[4,2,64,256]{3,2,1,0:T(8,128)(2,1)} %param.12) | copy-start | bytes 786436
  190.1 8.6 %copy-start.7 = (s32[16]{0:T(128)S(1)}, s32[16]{0:T(128)}, u32[]{:S(2)}) copy-start(s32[16]{0:T(128)} %param.15) | copy-start | bytes 196
  193.2 36.3 %all-to-all-start.1 = ((bf16[8,4,40,512]{3,2,1,0:T(8,128)(2,1)}), bf16[8,4,40,512]{3,2,1,0:T(8,128)(2,1)S(1)}, u32[]{:S(2)}, u32[]{:S(2)}) async-start(bf16[8,4,40,512]{3,2,1,0:T(8,128)(2,1)} %reshape.97), calls=%async_computation.2 | async-start | bytes 2621440 | tf_op jit(solution)/shard_map/all_to_all | solution.py:94
  263.8 1.7 copy-start.1
  268.1 1.2 copy-start.4
  268.1 2.4 copy-start.3
  268.1 2.8 copy-start.2
Sparse Core Ops, SparseCore 0:
  155.0 33.0 all-reduce.1
  190.7 71.2 reduce-scatter.1
where the time goes:
time: 279 us
  blocking collectives  129 us (46%)
  waiting for transfers between devices  71.1 us (25%)
  other arithmetic  26.2 us (9%)
  matrix products  17.9 us (6%)
  local copies, waits for them, and re-layouts  14.8 us (5%)
  between operations  14.2 us (5%)
  starting transfers between devices  5.78 us (2%)
    all_to_all x1, blocking collectives, local(): lax.all_to_all(send_rows, 'store', split_axis=0, concat_axis=0, tiled=True)  120 us
    all_to_all x1, waiting for transfers between devices, local(): lax.all_to_all(back_rows, 'store', split_axis=0, concat_axis=0, tiled=True)  27.2 us
    reduce_scatter x1, waiting for transfers between devices, local(): lax.psum_scatter(partial_value, 'tensor', scatter_dimension=2, tiled=True)  25.9 us
    psum x1, waiting for transfers between devices, local(): rank_total_sum = lax.psum(down_projected, 'tensor')  18.1 us
    dot_general x1, matrix products, local(): jnp.einsum('td,djk->tjk', normed, kv_weight, preferred_element_type=jnp.f...  14.9 us
    scatter x1, other arithmetic, local(): jnp.zeros((adapter_total * capacity, local_width), jnp.bfloat16).at[targets]  11.2 us
    psum x1, blocking collectives, local(): squares = lax.psum(jnp.sum(widened * widened, axis=1), 'tensor')  8.38 us
  transfers between devices with their start and end apart: 3, of which 3 were waited for; matrix products, arithmetic and copies ran while one was open for 11% of the time, Pallas kernels for 0%

commit v1 on v0

--- a/solution.py
+++ b/solution.py
@@ -82,7 +82,11 @@
         adapter_down,
         preferred_element_type=jnp.float32,
     )
-    rank_total_sum = lax.psum(down_projected, "tensor")
+    rank_total_sum = down_projected
+    for hop in (1, 2):
+        rank_total_sum = rank_total_sum + lax.ppermute(
+            rank_total_sum, "tensor", [(dev, dev ^ hop) for dev in range(4)]
+        )
     rank_activation = (rank_total_sum * adapter_scale).astype(jnp.bfloat16)
     split_rank = rank_activation.reshape(rank_activation.shape[:3] + (2, ADAPTER_RANK))
     update_rows = jnp.einsum(

time: 279 us -> 251 us (0.90)
  waiting for transfers between devices: 71.1 us -> 44.8 us
    reduce_scatter x1, waiting for transfers between devices: 25.9 us -> 0.02 us  [local(): lax.psum_scatter(partial_value, 'tensor', scatter_dimension=2, tiled=True)]
    psum x1 -> x0, waiting for transfers between devices: 18.1 us -> none  [local(): rank_total_sum = lax.psum(down_projected, 'tensor')]
    ppermute x0 -> x2, waiting for transfers between devices: none -> 17.3 us  [local(): lax.ppermute(rank_total_sum, 'tensor', [(dev, dev ^ hop) for dev in range...]
  transfers between devices with their start and end apart: 3 -> 4, of which waited for: 3 -> 3; matrix products, arithmetic and copies ran while one was open for 11% -> 12% of each run, Pallas kernels for 0% -> 0%
where the time goes in v1:
time: 251 us
  blocking collectives  129 us (51%)
  waiting for transfers between devices  44.8 us (18%)
  other arithmetic  24.9 us (10%)
  matrix products  17 us (7%)
  local copies, waits for them, and re-layouts  15.6 us (6%)
  between operations  14.3 us (6%)
  starting transfers between devices  5.32 us (2%)
    all_to_all x1, blocking collectives, local(): lax.all_to_all(send_rows, 'store', split_axis=0, concat_axis=0, tiled=True)  120 us
    all_to_all x1, waiting for transfers between devices, local(): lax.all_to_all(back_rows, 'store', split_axis=0, concat_axis=0, tiled=True)  27.4 us
    ppermute x2, waiting for transfers between devices, local(): lax.ppermute(rank_total_sum, 'tensor', [(dev, dev ^ hop) for dev in range...  17.3 us
    dot_general x1, matrix products, local(): jnp.einsum('td,djk->tjk', normed, kv_weight, preferred_element_type=jnp.f...  14.9 us
    scatter x1, other arithmetic, local(): jnp.zeros((adapter_total * capacity, local_width), jnp.bfloat16).at[targets]  12.2 us
    psum x1, blocking collectives, local(): squares = lax.psum(jnp.sum(widened * widened, axis=1), 'tensor')  8.38 us
    gather x1, local copies, waits for them, and re-layouts, local(): returned.reshape(adapter_total * capacity, 2, kv_local)[targets]  5.5 us
  transfers between devices with their start and end apart: 4, of which 3 were waited for; matrix products, arithmetic and copies ran while one was open for 12% of the time, Pallas kernels for 0%

profile of v1, /device:TPU:0, one launch (start us, length us, event | category | flops | bytes accessed | tf_op | source)
XLA Modules:
  0.0 250.5 jit_solution(16292247925499808871)
XLA Ops:
  7.2 3.2 %fusion = f32[1024]{0:T(1024)S(1)} fusion(bf16[1024,2048]{1,0:T(8,128)(2,1)} %param.8), kind=kLoop, calls=%fused_computation.4 | loop fusion | flops 6290432 | bytes 4198400 | tf_op jit(solution)/shard_map/reduce_sum | solution.py:70
  10.4 8.4 %psum.7 = f32[1024]{0:T(1024)S(1)} all-reduce(f32[1024]{0:T(1024)S(1)} %fusion), channel_id=1, replica_groups=mesh['store'=8,'tensor'=4] {'tensor'}, use_global_device_ids=true, to_apply=%region_1.0 | all-reduce | flops 1024 | bytes 8192 | tf_op jit(solution)/shard_map/psum | solution.py:70
  18.8 14.9 %fusion.3 = f32[1024,2,1024]{2,0,1:T(8,128)} fusion(bf16[2048,2,1024]{2,1,0:T(2,128)(2,1)} %param.10, bf16[1024,2048]{1,0:T(8,128)(2,1)} %param.8, f32[2048]{0:T(1024)S(1)} %copy-done.6, f32[1024]{0:T(1024)S(1)} %add_rsqrt_fusion), kind=kOutput, calls=%fused_computation.7 | convolution fusion | flops 8598323200 | bytes 20983808 | tf_op jit(solution)/shard_map/td,djk->tjk/dot_general | solution.py:100
  33.7 0.7 copy-done.7
  34.5 0.5 convert_reduce_fusion
  35.0 12.2 %scatter_custom_fusion = bf16[1280,2048]{1,0:T(8,128)(2,1)} fusion(s32[1024]{0:T(1024)S(1)} %bitcast.50, bf16[]{:T(256)} %constant.6.clone.1, bf16[1024,2048]{1,0:T(8,128)(2,1)} %param.8, f32[2048]{0:T(1024)S(1)} %copy-done.6, f32[1024]{0:T(1024)S(1)} %add_rsqrt_fusion), kind=kCustom, calls=%fused_computation.15 | custom fusion | flops 8388608 | bytes 9449474 | tf_op jit(solution)/shard_map/scatter | solution.py:76
  47.3 120.3 %all_to_all.10 = bf16[8,4,40,2048]{3,2,1,0:T(8,128)(2,1)S(1)} all-to-all(bf16[8,4,40,2048]{3,2,1,0:T(8,128)(2,1)} %bitcast.46), channel_id=1, replica_groups=mesh['store'=8,'tensor'=4] {'store'}, dimensions={0} | all-to-all | bytes 10485760 | tf_op jit(solution)/shard_map/all_to_all | solution.py:81
  167.5 1.7 fusion.13
  169.3 2.1 collective-permute-done
  171.4 0.1 add.65
  171.5 1.6 collective-permute-start.1
  173.1 15.2 %collective-permute-done.1 = f32[8,4,40,128]{3,2,0,1:T(8,128)S(1)} collective-permute-done((f32[8,4,40,128]{3,2,0,1:T(8,128)S(1)}, f32[8,4,40,128]{3,2,0,1:T(8,128)S(1)}, u32[]{:S(2)}, u32[]{:S(2)}) %collective-permute-start.1) | collective-permute-done | bytes 655392 | tf_op jit(solution)/shard_map/ppermute | solution.py:87
  188.4 0.3 reshape.96
  188.7 0.5 fusion.12
  189.2 1.3 copy.28
  190.6 1.7 reshape.97
  192.3 3.6 %all-to-all-start.1 = ((bf16[8,4,40,512]{3,2,1,0:T(8,128)(2,1)}), bf16[8,4,40,512]{3,2,1,0:T(8,128)(2,1)S(1)}, u32[]{:S(2)}, u32[]{:S(2)}) async-start(bf16[8,4,40,512]{3,2,1,0:T(8,128)(2,1)} %reshape.97), calls=%async_computation.2 | async-start | bytes 2621440 | tf_op jit(solution)/shard_map/all_to_all | solution.py:98
  196.0 0.1 reduce
  196.3 1.9 multiply_cosine_fusion
  198.2 1.3 pad_maximum_fusion
  199.5 27.4 %all-to-all-done.1 = bf16[8,4,40,512]{3,2,1,0:T(8,128)(2,1)S(1)} async-done(((bf16[8,4,40,512]{3,2,1,0:T(8,128)(2,1)}), bf16[8,4,40,512]{3,2,1,0:T(8,128)(2,1)S(1)}, u32[]{:S(2)}, u32[]{:S(2)}) %all-to-all-start.1) | async-done | bytes 1310752 | tf_op jit(solution)/shard_map/all_to_all | solution.py:98
  226.9 1.3 reshape.98
  228.2 5.5 %gather_fusion = bf16[1024,2,256]{2,1,0:T(2,128)(2,1)S(1)} fusion(bf16[1280,2,256]{2,1,0:T(2,128)(2,1)} %reshape.98, s32[1024]{0:T(1024)S(1)} %broadcast_clamp_fusion), kind=kCustom, calls=%fused_computation | custom fusion | bytes 2101248 | tf_op jit(solution)/shard_map/gather | solution.py:99
  233.8 1.8 convert_add_fusion
  235.6 1.1 slice.19
  236.7 0.5 copy-done.1
  237.2 0.8 fusion.22
  238.1 1.7 reshape_squeeze.6
  239.9 1.1 slice_negate_fusion
  241.0 1.2 maximum_multiply_fusion
  242.3 0.4 mul.103
  242.6 1.0 fusion.20
  (34 shorter events, 0.6 us)
Async XLA Ops:
  7.2 160.4 %copy-start = (bf16[4,2048,128]{2,1,0:T(8,128)(2,1)S(1)}, bf16[4,2048,128]{2,1,0:T(8,128)(2,1)}, u32[]{:S(2)}) copy-start(bf16[4,2048,128]{2,1,0:T(8,128)(2,1)} %param.11) | copy-start | bytes 6291460
  7.2 11.7 %copy-start.6 = (f32[2048]{0:T(1024)S(1)}, f32[2048]{0:T(1024)}, u32[]{:S(2)}) copy-start(f32[2048]{0:T(1024)} %param.9) | copy-start | bytes 24580
  7.2 226.6 %reduce-scatter.2.cloned.1.call-start = ((), (), s32[]{:S(2)}) async-start(), calls=%async_computation.3 | async-start | bytes 10485760 | tf_op jit(solution)/shard_map/reduce_scatter | solution.py:101
  33.7 0.7 copy-start.7
  33.7 0.7 copy-start.9
  169.2 19.5 %copy-start.5 = (bf16[4,2,64,256]{3,2,1,0:T(8,128)(2,1)S(1)}, bf16[4,2,64,256]{3,2,1,0:T(8,128)(2,1)}, u32[]{:S(2)}) copy-start(bf16[4,2,64,256]{3,2,1,0:T(8,128)(2,1)} %param.12) | copy-start | bytes 786436
  169.2 2.2 collective-permute-start
  171.5 16.8 %collective-permute-start.1 = (f32[8,4,40,128]{3,2,0,1:T(8,128)S(1)}, f32[8,4,40,128]{3,2,0,1:T(8,128)S(1)}, u32[]{:S(2)}, u32[]{:S(2)}) collective-permute-start(f32[8,4,40,128]{3,2,0,1:T(8,128)S(1)} %add.65), channel_id=1, source_target_pairs={{0,2},{1,3},{2,0},{3,1},{4,6},{5,7},{6,4},{7,5},{8,10},{9,11},{10,... | collective-permute-start | bytes 1966088 | tf_op jit(solution)/shard_map/ppermute | solution.py:87
  189.2 6.7 %copy-start.8 = (s32[16]{0:T(128)S(1)}, s32[16]{0:T(128)}, u32[]{:S(2)}) copy-start(s32[16]{0:T(128)} %param.15) | copy-start | bytes 196
  192.3 34.6 %all-to-all-start.1 = ((bf16[8,4,40,512]{3,2,1,0:T(8,128)(2,1)}), bf16[8,4,40,512]{3,2,1,0:T(8,128)(2,1)S(1)}, u32[]{:S(2)}, u32[]{:S(2)}) async-start(bf16[8,4,40,512]{3,2,1,0:T(8,128)(2,1)} %reshape.97), calls=%async_computation.2 | async-start | bytes 2621440 | tf_op jit(solution)/shard_map/all_to_all | solution.py:98
  235.6 1.7 copy-start.1
  239.8 1.2 copy-start.4
  239.8 2.4 copy-start.3
  239.9 2.8 %copy-start.2 = (f32[1024,2,256]{2,0,1:T(8,128)S(1)}, f32[1024,2,256]{2,0,1:T(8,128)}, u32[]{:S(2)}) copy-start(f32[1024,2,256]{2,0,1:T(8,128)} %copy-done.1) | copy-start | bytes 6291460
Sparse Core Ops, SparseCore 0:
  33.9 71.5 reduce-scatter.1
